TPU v7x, 512 devices: a whole 4x4x16 slice. The times are simulated.
512 devices in a mesh: dp: 8 (over x, core), expert: 64 (over y, z).
Axes of the slice: x: 4, y: 4, z: 16, core: 2. Of those that a mesh axis runs over, the one named last changes fastest.
Arguments:
- tokens: bfloat16 [8192, 2048], P('expert', 'dp'), may hold values from -6 to 6
- cotangent: bfloat16 [8192, 2048], P('expert', 'dp'), may hold values from -6 to 6
- routes: int32 [8192, 8], P('expert'), may hold values from 0 to 63, as said below
- mix_weights: float32 [8192, 8], P('expert'), may hold values from 0.05 to 0.5
- w_gate: bfloat16 [64, 2048, 384], P('expert', 'dp'), may hold values from -0.125 to 0.125
- w_up: bfloat16 [64, 2048, 384], P('expert', 'dp'), may hold values from -0.125 to 0.125
- w_down: bfloat16 [64, 384, 2048], P('expert', None, 'dp'), may hold values from -0.3125 to 0.3125
Outputs:
- mixed: bfloat16 [8192, 2048], P('expert', 'dp')
- token_grad: bfloat16 [8192, 2048], P('expert', 'dp')
- gate_grad: float32 [64, 2048, 384], P('expert', 'dp')
- up_grad: float32 [64, 2048, 384], P('expert', 'dp')
- down_grad: float32 [64, 384, 2048], P('expert', None, 'dp')
Inputs may be any that keep to these rules, and one draw needn't show every extreme that they name: `routes`: each row names 8 different experts. In each aligned block of 128 rows at most 32 rows name the same expert, and some block reaches that. In all, at most 1792 rows name one expert, and some expert is named by exactly that many.
All inputs are finite; a program needn't handle non-finite values.
Results may differ from a plain program's by a relative error of at most 0.023.
Values may be sent and summed in bfloat16 or wider, within the bound.
A program may use at most 64 MiB of HBM per device.

v0:
```python
import jax
import jax.numpy as jnp
from jax import lax
from jax.sharding import PartitionSpec as P


def contract(left_side, right_side, left_dim, right_dim):
    return lax.dot_general(
        left_side,
        right_side,
        (((left_dim,), (right_dim,)), ((), ())),
        preferred_element_type=jnp.float32,
    )


def silu_parts(gate_in):
    logistic = jax.nn.sigmoid(gate_in)
    return (gate_in * logistic, logistic * (1.0 + gate_in * (1.0 - logistic)))


def split_three(values):
    high = values.astype(jnp.bfloat16)
    rest = values - high.astype(jnp.float32)
    middle = rest.astype(jnp.bfloat16)
    low = (rest - middle.astype(jnp.float32)).astype(jnp.bfloat16)
    return (high, middle, low)


def shards(tokens, cotangent, routes, mix_weights, w_gate, w_up, w_down):
    tok_rows, width_dev = tokens.shape
    picks_per = routes.shape[1]
    dp_count = lax.axis_size("dp")
    owner_count = lax.axis_size("expert")
    hidden = w_gate.shape[2]
    sub_rows = tok_rows // dp_count
    width = width_dev * dp_count
    me_dp = lax.axis_index("dp")
    me_expert = lax.axis_index("expert")
    weights_dev = jnp.concatenate([w_gate[0], w_up[0], w_down[0].T], axis=1)
    weights = lax.all_gather(weights_dev, "dp", axis=0, tiled=True)
    both = jnp.stack([tokens, cotangent]).reshape(2, dp_count, sub_rows, width_dev)
    both = lax.all_to_all(both, "dp", split_axis=1, concat_axis=1, tiled=True)
    both = both.transpose(2, 0, 1, 3).reshape(sub_rows, 2 * width)
    my_routes = lax.dynamic_slice_in_dim(routes, me_dp * sub_rows, sub_rows, 0)
    my_mix = lax.dynamic_slice_in_dim(mix_weights, me_dp * sub_rows, sub_rows, 0)
    extra = jnp.concatenate([my_routes.astype(jnp.bfloat16), *split_three(my_mix)], axis=1)
    extra = jnp.pad(extra, ((0, 0), (0, 128 - extra.shape[1])))
    rows = lax.all_gather(jnp.concatenate([both, extra], axis=1), "expert", axis=0, tiled=True)
    x_rows = rows[:, :width]
    c_rows = rows[:, width : 2 * width]
    tail = rows[:, 2 * width : 2 * width + 4 * picks_per].astype(jnp.float32)
    tail = tail.reshape(-1, 4, picks_per)
    mix_all = tail[:, 1] + tail[:, 2] + tail[:, 3]
    named = tail[:, 0] == me_expert.astype(jnp.float32)
    weight_row = jnp.sum(jnp.where(named, mix_all, 0.0), axis=1, keepdims=True)
    w_in = weights[:, : 2 * hidden]
    w_out = weights[:, 2 * hidden :]
    pre = contract(x_rows, w_in, 1, 0)
    back_hidden = contract(c_rows, w_out, 1, 0) * weight_row
    gate_in, up_in = (pre[:, :hidden], pre[:, hidden:])
    activated, slope_silu = silu_parts(gate_in)
    hidden_mix = (activated * up_in * weight_row).astype(jnp.bfloat16)
    gate_back = (back_hidden * up_in * slope_silu).astype(jnp.bfloat16)
    up_back = (back_hidden * activated).astype(jnp.bfloat16)
    in_back = jnp.concatenate([gate_back, up_back], axis=1)
    mixed_part = contract(hidden_mix, w_out, 1, 1).astype(jnp.bfloat16)
    grad_part = contract(in_back, w_in, 1, 1).astype(jnp.bfloat16)
    sums = lax.psum_scatter(
        jnp.concatenate([mixed_part, grad_part], axis=1), "expert", scatter_dimension=0, tiled=True
    )
    in_grad = contract(x_rows, in_back, 0, 0).astype(jnp.bfloat16)
    out_grad = contract(c_rows, hidden_mix, 0, 0).astype(jnp.bfloat16)
    weight_grads = lax.psum_scatter(
        jnp.concatenate([in_grad, out_grad], axis=1), "dp", scatter_dimension=0, tiled=True
    ).astype(jnp.float32)
    sums = sums.reshape(sub_rows, 2, dp_count, width_dev).transpose(1, 2, 0, 3)
    sums = lax.all_to_all(sums, "dp", split_axis=1, concat_axis=1, tiled=True)
    sums = sums.reshape(2, tok_rows, width_dev)
    return (
        sums[0],
        sums[1],
        weight_grads[None, :, :hidden],
        weight_grads[None, :, hidden : 2 * hidden],
        weight_grads[:, 2 * hidden :].T[None],
    )


def solution(mesh):
    placed = (
        P("expert", "dp"),
        P("expert", "dp"),
        P("expert", None),
        P("expert", None),
        P("expert", "dp", None),
        P("expert", "dp", None),
        P("expert", None, "dp"),
    )
    return jax.shard_map(
        shards,
        mesh=mesh,
        in_specs=placed,
        out_specs=(
            P("expert", "dp"),
            P("expert", "dp"),
            P("expert", "dp", None),
            P("expert", "dp", None),
            P("expert", None, "dp"),
        ),
        check_vma=False,
    )
```

profile of v0, /device:TPU:1, one launch (start us, length us, event | category | flops | bytes accessed | tf_op | source)
XLA Modules:
  0.0 1037.5 jit_solution(6336059974394394952)
XLA Ops:
  7.2 0.9 pad_maximum_fusion.6
  8.1 0.8 copy.61
  8.8 10.1 all-to-all-start
  19.0 0.0 all-gather.3.cloned.1.call-start
  19.0 0.8 subtract_convert_fusion
  19.8 0.8 dynamic-slice_convert_fusion
  20.6 0.1 copy.75
  20.7 3.6 all-to-all-done
  24.2 0.1 copy.62
  24.4 0.7 fusion.23
  25.0 0.0 all-gather.3.cloned.1.call-update
  25.0 0.0 all-gather.5.cloned.1.call-start
  25.1 1.1 copy.64
  26.2 1.1 copy.65
  27.2 1.8 pad_maximum_fusion.5
  29.0 0.0 all-gather.5.cloned.1.call-update
  29.1 0.0 reduce-scatter.5.cloned.1.call-start
  29.1 143.9 %all-gather.3.cloned.1.call-done = bf16[1024,4224]{1,0:T(8,128)(2,1)} async-done(((bf16[16,4224]{1,0:T(8,128)(2,1)}), bf16[1024,4224]{1,0:T(8,128)(2,1)}) %all-gather.3.cloned.1.call-update) | async-done | bytes 8650768 | tf_op jit(solution)/shard_map/all_gather | solution.py:48
  173.1 1.0 slice.70
  174.0 0.1 copy.72
  174.2 49.0 %all-gather.5.cloned.1.call-done = bf16[2048,1152]{0,1:T(8,128)(2,1)} async-done(((bf16[256,1152]{0,1:T(8,128)(2,1)}), bf16[2048,1152]{0,1:T(8,128)(2,1)}) %all-gather.5.cloned.1.call-update) | async-done | bytes 4718608 | tf_op jit(solution)/shard_map/all_gather | solution.py:40
  223.2 0.0 slice-start
  223.2 0.0 slice-start.1
  223.2 6.3 fusion.6
  229.5 0.0 slice-start.2
  229.5 5.2 multiply_convert_fusion.1
  234.7 0.0 slice-done
  234.7 0.0 slice-done.1
  234.7 0.0 slice-done.2
  234.7 1.8 fusion.11
  236.5 3.6 fusion.8
  240.2 2.5 pad_maximum_fusion.1
  242.7 0.0 reduce-scatter.5.cloned.1.call-update
  242.7 0.2 reduce-scatter.3.cloned.1.call-start
  242.9 5.8 convolution_convert_fusion
  248.7 6.9 convolution_convert_fusion.1
  255.7 7.9 pad_maximum_fusion
  263.6 0.0 reduce-scatter.3.cloned.1.call-update
  263.6 24.4 %reduce-scatter.5.cloned.1.call-done = bf16[256,1152]{0,1:T(8,128)(2,1)} async-done(((bf16[2048,1152]{0,1:T(8,128)(2,1)}), bf16[256,1152]{0,1:T(8,128)(2,1)}) %reduce-scatter.5.cloned.1.call-update) | async-done | bytes 589840 | tf_op jit(solution)/shard_map/reduce_scatter | solution.py:73
  288.1 1.1 convert_element_type.62
  289.2 718.3 %reduce-scatter.3.cloned.1.call-done = bf16[16,4096]{1,0:T(8,128)(2,1)} async-done(((bf16[1024,4096]{1,0:T(8,128)(2,1)}), bf16[16,4096]{1,0:T(8,128)(2,1)}) %reduce-scatter.3.cloned.1.call-update) | async-done | bytes 131088 | tf_op jit(solution)/shard_map/reduce_scatter | solution.py:68
  1007.5 0.9 copy.77
  1008.5 0.8 copy.79
  1009.2 15.0 %all-to-all-start.1 = ((bf16[2,8,16,256]{3,0,2,1:T(2,128)(2,1)}), bf16[2,8,16,256]{3,0,2,1:T(2,128)(2,1)S(1)}, u32[]{:S(2)}, u32[]{:S(2)}) async-start(bf16[2,8,16,256]{3,0,2,1:T(2,128)(2,1)} %bitcast.31), calls=%async_computation.2 | async-start | bytes 262144 | tf_op jit(solution)/shard_map/all_to_all | solution.py:77
  1024.2 0.8 slice_bitcast_fusion
  1025.1 0.9 copy.71
  1026.0 0.9 copy.70
  1026.9 2.6 all-to-all-done.1
  1029.5 0.2 fusion.30
  1029.7 0.6 copy.74
  1030.4 0.6 copy.73
  (5 shorter events, 0.1 us)
Async XLA Ops:
  8.8 15.4 %all-to-all-start = ((bf16[2,8,16,256]{3,0,2,1:T(2,128)(2,1)}), bf16[2,8,16,256]{3,0,2,1:T(2,128)(2,1)S(1)}, u32[]{:S(2)}, u32[]{:S(2)}) async-start(bf16[2,8,16,256]{3,0,2,1:T(2,128)(2,1)} %copy.61), calls=%async_computation | async-start | bytes 262144 | tf_op jit(solution)/shard_map/all_to_all | solution.py:42
  19.0 154.1 %all-gather.3.cloned.1.call-start = ((), (), s32[]{:S(2)}) async-start(), calls=%async_computation.4 | async-start | bytes 8785920 | tf_op jit(solution)/shard_map/all_gather | solution.py:48
  25.0 198.1 %all-gather.5.cloned.1.call-start = ((), (), s32[]{:S(2)}) async-start(), calls=%async_computation.5 | async-start | bytes 5308416 | tf_op jit(solution)/shard_map/all_gather | solution.py:40
  29.1 259.0 %reduce-scatter.5.cloned.1.call-start = ((), (), s32[]{:S(2)}) async-start(), calls=%async_computation.7 | async-start | bytes 5308416 | tf_op jit(solution)/shard_map/reduce_scatter | solution.py:73
  223.2 11.5 %slice-start = ((s8[8650752]{0:T(1024)(128)(4,1)}), s8[4194304]{0:T(1024)(128)(4,1)S(1)}, s32[]{:S(2)}) async-start(s8[8650752]{0:T(1024)(128)(4,1)} %bitcast.44), calls=%async_computation.8 | async-start | bytes 8388608
  223.2 11.5 %slice-start.1 = ((s8[8650752]{0:T(1024)(128)(4,1)}), s8[4194304]{0:T(1024)(128)(4,1)S(1)}, s32[]{:S(2)}) async-start(s8[8650752]{0:T(1024)(128)(4,1)} %bitcast.44), calls=%async_computation.9 | async-start | bytes 8388608
  229.5 5.2 slice-start.2
  242.7 764.8 %reduce-scatter.3.cloned.1.call-start = ((), (), s32[]{:S(2)}) async-start(), calls=%async_computation.6 | async-start | bytes 8519680 | tf_op jit(solution)/shard_map/reduce_scatter | solution.py:68
  1009.2 20.3 %all-to-all-start.1 = ((bf16[2,8,16,256]{3,0,2,1:T(2,128)(2,1)}), bf16[2,8,16,256]{3,0,2,1:T(2,128)(2,1)S(1)}, u32[]{:S(2)}, u32[]{:S(2)}) async-start(bf16[2,8,16,256]{3,0,2,1:T(2,128)(2,1)} %bitcast.31), calls=%async_computation.2 | async-start | bytes 262144 | tf_op jit(solution)/shard_map/all_to_all | solution.py:77
Sparse Core Ops, SparseCore 0:
  25.2 147.8 all-gather.2
  175.2 47.9 all-gather.4
  242.8 45.1 reduce-scatter.4
  292.4 715.1 reduce-scatter.2
where the time goes:
time: 1040 us
  waiting for transfers between devices  942 us (91%)
  matrix products  29.7 us (3%)
  starting transfers between devices  25.4 us (2%)
  other arithmetic  16.6 us (2%)
  between operations  13.9 us (1%)
    reduce_scatter x1, waiting for transfers between devices, shards(): lax.psum_scatter(jnp.concatenate([mixed_part, grad_part], axis=1), 'exper...  718 us
    all_gather x1, waiting for transfers between devices, shards(): lax.all_gather(jnp.concatenate([both, extra], axis=1), 'expert', axis=0,...  144 us
    all_gather x1, waiting for transfers between devices, shards(): weights = lax.all_gather(weights_dev, 'dp', axis=0, tiled=True)  49 us
    dot_general x6, matrix products, contract(): lax.dot_general(left_side, right_side, (((left_dim,), (right_dim,)), ((),...  29.7 us
    reduce_scatter x1, waiting for transfers between devices, shards(): lax.psum_scatter(jnp.concatenate([in_grad, out_grad], axis=1), 'dp', scat...  24.4 us
  transfers between devices with their start and end apart: 6, of which 6 were waited for; matrix products, arithmetic and copies ran while one was open for 3% of the time, Pallas kernels for 0%

commit v1 on v0

--- a/solution.py
+++ b/solution.py
@@ -1,7 +1,17 @@
+import functools
 import jax
 import jax.numpy as jnp
 from jax import lax
 from jax.sharding import PartitionSpec as P
+
+
+def sectors_group(u_in, on_dim):
+    shaped = jax.lax.psum(1, "expert")
+    field_out = jnp.stack([u_in] * shaped)
+    return jnp.concatenate(jax.lax.all_to_all(field_out, "expert", 0, 0), on_dim)
+
+
+ways_draw = functools.partial(sectors_group, on_dim=0)
 
 
 def contract(left_side, right_side, left_dim, right_dim):
@@ -45,7 +55,7 @@
     my_mix = lax.dynamic_slice_in_dim(mix_weights, me_dp * sub_rows, sub_rows, 0)
     extra = jnp.concatenate([my_routes.astype(jnp.bfloat16), *split_three(my_mix)], axis=1)
     extra = jnp.pad(extra, ((0, 0), (0, 128 - extra.shape[1])))
-    rows = lax.all_gather(jnp.concatenate([both, extra], axis=1), "expert", axis=0, tiled=True)
+    rows = ways_draw(jnp.concatenate([both, extra], axis=1))
     x_rows = rows[:, :width]
     c_rows = rows[:, width : 2 * width]
     tail = rows[:, 2 * width : 2 * width + 4 * picks_per].astype(jnp.float32)

time: 1040 us -> 1230 us (1.18)
  waiting for transfers between devices: 942 us -> 1120 us
  starting transfers between devices: 25.4 us -> 39.9 us
    all_to_all x0 -> x1, waiting for transfers between devices: none -> 376 us  [sectors_group(): jax.lax.all_to_all(field_out, 'expert', 0, 0)]
    all_gather x1 -> x0, waiting for transfers between devices: 144 us -> none  [shards(): lax.all_gather(jnp.concatenate([both, extra], axis=1), 'expert', axis=0,...]
    all_gather x1, waiting for transfers between devices: 49 us -> 0.02 us  [shards(): weights = lax.all_gather(weights_dev, 'dp', axis=0, tiled=True)]
    all_to_all x0 -> x1, starting transfers between devices: none -> 14.5 us  [sectors_group(): jax.lax.all_to_all(field_out, 'expert', 0, 0)]
  transfers between devices with their start and end apart: 6 -> 6, of which waited for: 6 -> 5; matrix products, arithmetic and copies ran while one was open for 3% -> 2% of each run, Pallas kernels for 0% -> 0%
where the time goes in v1:
time: 1230 us
  waiting for transfers between devices  1120 us (91%)
  starting transfers between devices  39.9 us (3%)
  matrix products  34.6 us (3%)
  other arithmetic  15.1 us (1%)
  between operations  13.9 us (1%)
    reduce_scatter x1, waiting for transfers between devices, shards(): lax.psum_scatter(jnp.concatenate([mixed_part, grad_part], axis=1), 'exper...  719 us
    all_to_all x1, waiting for transfers between devices, sectors_group(): jax.lax.all_to_all(field_out, 'expert', 0, 0)  376 us
    dot_general x6, matrix products, contract(): lax.dot_general(left_side, right_side, (((left_dim,), (right_dim,)), ((),...  34.6 us
  transfers between devices with their start and end apart: 6, of which 5 were waited for; matrix products, arithmetic and copies ran while one was open for 2% of the time, Pallas kernels for 0%

profile of v1, /device:TPU:1, one launch (start us, length us, event | category | flops | bytes accessed | tf_op | source)
XLA Modules:
  0.0 1233.6 jit_solution(4600604086334493116)
XLA Ops:
  7.2 0.9 pad_maximum_fusion.6
  8.1 0.8 copy.62
  8.8 10.1 all-to-all-start
  19.0 0.8 subtract_convert_fusion
  19.8 0.8 dynamic-slice_convert_fusion
  20.6 0.1 copy.76
  20.6 3.6 all-to-all-done
  24.2 0.1 copy.63
  24.4 3.9 stack.11
  28.3 0.0 copy-start.1
  28.3 0.0 copy-start.2
  28.3 0.0 copy-start
  28.3 14.5 %all-to-all-start.1 = ((bf16[64,16,4224]{2,1,0:T(8,128)(2,1)}), bf16[64,16,4224]{2,1,0:T(8,128)(2,1)}, u32[]{:S(2)}, u32[]{:S(2)}) async-start(bf16[64,16,4224]{2,1,0:T(8,128)(2,1)} %stack.11), calls=%async_computation.1 | async-start | bytes 17301504 | tf_op jit(solution)/shard_map/all_to_all | solution.py:11
  42.8 0.0 all-gather.2.cloned.1.call-start
  42.8 0.0 copy-done.1
  42.8 0.1 copy.65
  43.0 0.0 copy-done.2
  43.0 0.1 copy.66
  43.1 0.0 copy-done
  43.1 0.9 pad_maximum_fusion.5
  44.0 0.0 all-gather.2.cloned.1.call-update
  44.1 0.0 reduce-scatter.5.cloned.1.call-start
  44.1 375.9 %all-to-all-done.1 = bf16[64,16,4224]{2,1,0:T(8,128)(2,1)} async-done(((bf16[64,16,4224]{2,1,0:T(8,128)(2,1)}), bf16[64,16,4224]{2,1,0:T(8,128)(2,1)}, u32[]{:S(2)}, u32[]{:S(2)}) %all-to-all-start.1) | async-done | bytes 8650784 | tf_op jit(solution)/shard_map/all_to_all | solution.py:11
  420.0 1.0 slice.70
  421.0 0.1 copy.73
  421.2 0.0 all-gather.2.cloned.1.call-done
  421.2 6.2 fusion.6
  427.4 5.1 multiply_convert_fusion.1
  432.5 4.0 fusion.11
  436.5 6.5 fusion.8
  443.0 2.6 pad_maximum_fusion.1
  445.6 0.0 reduce-scatter.5.cloned.1.call-update
  445.6 0.2 reduce-scatter.3.cloned.1.call-start
  445.8 5.9 convolution_convert_fusion
  451.7 6.9 convolution_convert_fusion.1
  458.6 7.9 pad_maximum_fusion
  466.5 0.0 reduce-scatter.3.cloned.1.call-update
  466.6 17.1 %reduce-scatter.5.cloned.1.call-done = bf16[256,1152]{0,1:T(8,128)(2,1)} async-done(((bf16[2048,1152]{0,1:T(8,128)(2,1)}), bf16[256,1152]{0,1:T(8,128)(2,1)}) %reduce-scatter.5.cloned.1.call-update) | async-done | bytes 589840 | tf_op jit(solution)/shard_map/reduce_scatter | solution.py:83
  483.7 1.1 convert_element_type.62
  484.8 718.7 %reduce-scatter.3.cloned.1.call-done = bf16[16,4096]{1,0:T(8,128)(2,1)} async-done(((bf16[1024,4096]{1,0:T(8,128)(2,1)}), bf16[16,4096]{1,0:T(8,128)(2,1)}) %reduce-scatter.3.cloned.1.call-update) | async-done | bytes 131088 | tf_op jit(solution)/shard_map/reduce_scatter | solution.py:78
  1203.6 0.9 copy.78
  1204.5 0.8 copy.80
  1205.3 15.0 %all-to-all-start.2 = ((bf16[2,8,16,256]{3,0,2,1:T(2,128)(2,1)}), bf16[2,8,16,256]{3,0,2,1:T(2,128)(2,1)S(1)}, u32[]{:S(2)}, u32[]{:S(2)}) async-start(bf16[2,8,16,256]{3,0,2,1:T(2,128)(2,1)} %bitcast.32), calls=%async_computation.3 | async-start | bytes 262144 | tf_op jit(solution)/shard_map/all_to_all | solution.py:87
  1220.3 0.8 slice_bitcast_fusion
  1221.1 0.9 copy.71
  1222.0 0.9 copy.72
  1222.9 2.6 all-to-all-done.2
  1225.5 0.2 fusion.30
  1225.8 0.6 copy.74
  1226.4 0.6 copy.75
  (5 shorter events, 0.1 us)
Async XLA Ops:
  8.8 15.4 %all-to-all-start = ((bf16[2,8,16,256]{3,0,2,1:T(2,128)(2,1)}), bf16[2,8,16,256]{3,0,2,1:T(2,128)(2,1)S(1)}, u32[]{:S(2)}, u32[]{:S(2)}) async-start(bf16[2,8,16,256]{3,0,2,1:T(2,128)(2,1)} %copy.62), calls=%async_computation | async-start | bytes 262144 | tf_op jit(solution)/shard_map/all_to_all | solution.py:52
  28.3 14.5 %copy-start.1 = (bf16[1,256,384]{2,1,0:T(8,128)(2,1)S(1)}, bf16[1,256,384]{2,1,0:T(8,128)(2,1)}, u32[]{:S(2)}) copy-start(bf16[1,256,384]{2,1,0:T(8,128)(2,1)} %param.11) | copy-start | bytes 589828
  28.3 14.7 %copy-start.2 = (bf16[1,256,384]{2,1,0:T(8,128)(2,1)S(1)}, bf16[1,256,384]{2,1,0:T(8,128)(2,1)}, u32[]{:S(2)}) copy-start(bf16[1,256,384]{2,1,0:T(8,128)(2,1)} %param.12) | copy-start | bytes 589828
  28.3 14.8 %copy-start = (bf16[1,384,256]{2,1,0:T(8,128)(2,1)S(1)}, bf16[1,384,256]{2,1,0:T(8,128)(2,1)}, u32[]{:S(2)}) copy-start(bf16[1,384,256]{2,1,0:T(8,128)(2,1)} %param.13) | copy-start | bytes 589828
  28.3 391.7 %all-to-all-start.1 = ((bf16[64,16,4224]{2,1,0:T(8,128)(2,1)}), bf16[64,16,4224]{2,1,0:T(8,128)(2,1)}, u32[]{:S(2)}, u32[]{:S(2)}) async-start(bf16[64,16,4224]{2,1,0:T(8,128)(2,1)} %stack.11), calls=%async_computation.1 | async-start | bytes 17301504 | tf_op jit(solution)/shard_map/all_to_all | solution.py:11
  42.8 378.4 %all-gather.2.cloned.1.call-start = ((), (), s32[]{:S(2)}) async-start(), calls=%async_computation.5 | async-start | bytes 5308416 | tf_op jit(solution)/shard_map/all_gather | solution.py:50
  44.1 439.6 %reduce-scatter.5.cloned.1.call-start = ((), (), s32[]{:S(2)}) async-start(), calls=%async_computation.7 | async-start | bytes 5308416 | tf_op jit(solution)/shard_map/reduce_scatter | solution.py:83
  445.6 758.0 %reduce-scatter.3.cloned.1.call-start = ((), (), s32[]{:S(2)}) async-start(), calls=%async_computation.6 | async-start | bytes 8519680 | tf_op jit(solution)/shard_map/reduce_scatter | solution.py:78
  1205.3 20.2 %all-to-all-start.2 = ((bf16[2,8,16,256]{3,0,2,1:T(2,128)(2,1)}), bf16[2,8,16,256]{3,0,2,1:T(2,128)(2,1)S(1)}, u32[]{:S(2)}, u32[]{:S(2)}) async-start(bf16[2,8,16,256]{3,0,2,1:T(2,128)(2,1)} %bitcast.32), calls=%async_computation.3 | async-start | bytes 262144 | tf_op jit(solution)/shard_map/all_to_all | solution.py:87
Sparse Core Ops, SparseCore 0:
  45.7 45.2 all-gather.1
  445.7 37.9 reduce-scatter.4
  488.2 715.3 reduce-scatter.2
